TPU v7x, 128 devices: a whole 4x4x4 slice. The times are simulated.
128 devices in a mesh: gx: 4 (over y), gy: 4 (over x), gz: 8 (over z, core).
Axes of the slice: x: 4, y: 4, z: 4, core: 2. Of those that a mesh axis runs over, the one named last changes fastest.
Arguments:
- token_grad: bfloat16 [131072, 320], P(('gx', 'gy', 'gz')), may hold values from -6 to 6
- token_owner: int32 [131072, 1], P(('gx', 'gy', 'gz')), may hold values from 0 to 127; in each aligned block of 1024 rows (0 to 1023, 1024 to 2047, ...) at most 16 rows name the same one
- token_row: int32 [131072], P(('gx', 'gy', 'gz')), may hold values from 0 to 4095
- table: float32 [524288, 320], P(('gx', 'gy', 'gz')), may hold values from -6 to 6
- accum: float32 [524288], P(('gx', 'gy', 'gz')), may hold values from 0.1 to 10
Outputs:
- new_table: float32 [524288, 320], P(('gx', 'gy', 'gz'))
- new_accum: float32 [524288], P(('gx', 'gy', 'gz'))
- fresh_rows: bfloat16 [131072, 320], P(('gx', 'gy', 'gz'))
Inputs may be any that keep to these rules, and one draw needn't show every extreme that they name: `token_owner`: among the 1024 tokens of one device no owner is named by more than 16 tokens.
All inputs are finite; a program needn't handle non-finite values.
Results may differ from a plain program's by a relative error of at most 0.001.
Values may be sent and summed in bfloat16 or wider, within the bound.
No kernel may reach another device: no remote copies, remote signals or barrier semaphores. Data moves between devices by JAX's collectives and lax.ppermute only.
A program may use at most 64 MiB of HBM per device.

v0:
```python
import jax
import jax.numpy as jnp
from jax import lax
from jax.sharding import PartitionSpec as P


def in_blocks(value, dim, count):
    before, after = (value.shape[:dim], value.shape[dim + 1 :])
    return jnp.moveaxis(value.reshape(*before, count, -1, *after), dim, 0)


def laid_out(blocks, dim):
    blocks = jnp.moveaxis(blocks, 0, dim)
    lengths = blocks.shape
    return blocks.reshape(*lengths[:dim], lengths[dim] * lengths[dim + 1], *lengths[dim + 2 :])


def joined_exchange(value, axis, axes, splits, concats):
    sizes = [lax.axis_size(a) for a in axes]
    blocks = in_blocks(value, splits[0], sizes[0])
    blocks = jnp.moveaxis(in_blocks(blocks, splits[1] + 1, sizes[1]), 0, 1)
    inside = blocks.shape[2:]
    blocks = blocks.reshape(-1, *inside)
    blocks = lax.all_to_all(blocks, axis, split_axis=0, concat_axis=0, tiled=True)
    blocks = laid_out(blocks.reshape(*sizes, *inside), concats[0] + 1)
    return laid_out(blocks, concats[1])


def body(token_grad, token_owner, token_row, table, accum):
    devices = lax.axis_size(("gx", "gy", "gz"))
    token_count = token_grad.shape[0]
    width = token_grad.shape[1]
    rows_dev = table.shape[0]
    capacity = max(2, 2 * token_count // devices)
    slot_count = devices * capacity
    owners = token_owner[:, 0]
    matches = owners[:, None] == jnp.arange(devices, dtype=jnp.int32)[None, :]
    earlier = (jnp.arange(token_count)[:, None] > jnp.arange(token_count)[None, :]).astype(
        jnp.bfloat16
    )
    before = jnp.dot(earlier, matches.astype(jnp.bfloat16), preferred_element_type=jnp.float32)
    order_rank = jnp.sum(jnp.where(matches, before, 0.0), axis=1).astype(jnp.int32)
    target = owners * capacity + order_rank
    placer = jnp.arange(slot_count, dtype=jnp.int32)[:, None] == target[None, :]
    placer_bf = placer.astype(jnp.bfloat16)
    send_grad = jnp.dot(placer_bf, token_grad, preferred_element_type=jnp.float32).astype(
        jnp.bfloat16
    )
    send_row = jnp.max(jnp.where(placer, token_row[None, :], -1), axis=1)
    depth_count = lax.axis_size("gz")
    plane_count = devices // depth_count
    recv_grad, recv_row = (
        joined_exchange(
            send_grad.reshape(plane_count, depth_count, capacity, width),
            ("gx", "gy", "gz"),
            (("gx", "gy"), "gz"),
            (0, 1),
            (0, 1),
        ),
        joined_exchange(
            send_row.reshape(plane_count, depth_count, capacity),
            ("gx", "gy", "gz"),
            (("gx", "gy"), "gz"),
            (0, 1),
            (0, 1),
        ),
    )
    recv_grad = recv_grad.reshape(slot_count, width)
    recv_row = recv_row.reshape(slot_count)
    onehot = (jnp.arange(rows_dev, dtype=jnp.int32)[:, None] == recv_row[None, :]).astype(
        jnp.bfloat16
    )
    grad_sum = jnp.dot(onehot, recv_grad, preferred_element_type=jnp.float32)
    new_accum = accum + jnp.mean(grad_sum * grad_sum, axis=1)
    new_table = table - 0.5 * grad_sum / (jnp.sqrt(new_accum) + 1e-08)[:, None]
    answer_rows = jnp.take(new_table, jnp.maximum(recv_row, 0), axis=0).astype(jnp.bfloat16)
    returned = joined_exchange(
        answer_rows.reshape(plane_count, depth_count, capacity, width),
        ("gx", "gy", "gz"),
        (("gx", "gy"), "gz"),
        (0, 1),
        (0, 1),
    )
    returned = returned.reshape(slot_count, width)
    fresh_rows = jnp.dot(placer_bf.T, returned, preferred_element_type=jnp.float32).astype(
        jnp.bfloat16
    )
    return (new_table, new_accum, fresh_rows)


def solution(mesh):
    return jax.shard_map(
        body,
        mesh=mesh,
        in_specs=(
            P(("gx", "gy", "gz"), None),
            P(("gx", "gy", "gz"), None),
            P(("gx", "gy", "gz")),
            P(("gx", "gy", "gz"), None),
            P(("gx", "gy", "gz")),
        ),
        out_specs=(P(("gx", "gy", "gz"), None), P(("gx", "gy", "gz")), P(("gx", "gy", "gz"), None)),
        check_vma=False,
    )
```

profile of v0, /device:TPU:1, one launch (start us, length us, event | category | flops | bytes accessed | tf_op | source)
XLA Modules:
  0.0 114.0 jit_solution(4630655157146922252)
XLA Ops:
  0.6 0.0 copy-start
  0.6 1.4 %fusion.10 = f32[1024]{0:T(1024)S(1)} fusion(s32[1024]{0:T(1024)} %bitcast.54), kind=kOutput, calls=%fused_computation.18 | convolution fusion | flops 270007296 | bytes 8192 | tf_op jit(solution)/shard_map/dot_general | solution.py:41
  2.0 0.7 convert_add_fusion
  2.7 1.9 %select_reduce_fusion = s32[2048]{0:T(1024)S(1)} fusion(s32[1024]{0:T(1024)} %param.7, s32[1024]{0:T(1024)S(1)} %convert_add_fusion), kind=kLoop, calls=%fused_computation.4 | loop fusion | flops 6289408 | bytes 16384 | tf_op jit(solution)/shard_map/reduce_max | solution.py:49
  4.6 0.7 reshape_transpose_transpose_reshape_reshape_reshape.7
  5.3 11.5 %all-to-all-start = ((s32[128,1,1,16]{3,2,1,0:T(1,128)}), s32[128,1,1,16]{3,2,1,0:T(1,128)S(1)}, u32[]{:S(2)}, u32[]{:S(2)}) async-start(s32[128,1,1,16]{3,2,1,0:T(1,128)} %bitcast.1), calls=%async_computation | async-start | bytes 131072 | tf_op jit(solution)/shard_map/all_to_all | solution.py:24
  16.8 0.0 copy-done
  16.8 1.8 %fusion.7 = bf16[2048,320]{0,1:T(8,128)(2,1)S(1)} fusion(bf16[1024,320]{0,1:T(8,128)(2,1)S(1)} %copy-done, s32[1024]{0:T(1024)S(1)} %convert_add_fusion), kind=kOutput, calls=%fused_computation.15 | convolution fusion | flops 1344929792 | bytes 1970176 | tf_op jit(solution)/shard_map/dot_general | solution.py:46
  18.6 1.6 %copy.17 = bf16[2048,320]{1,0:T(8,128)(2,1)} copy(bf16[2048,320]{0,1:T(8,128)(2,1)S(1)} %fusion.7) | data formatting | bytes 2621440 | tf_op jit(solution)/shard_map/convert_element_type | solution.py:46
  20.2 6.0 %all-to-all-done = s32[128,1,1,16]{3,2,1,0:T(1,128)S(1)} async-done(((s32[128,1,1,16]{3,2,1,0:T(1,128)}), s32[128,1,1,16]{3,2,1,0:T(1,128)S(1)}, u32[]{:S(2)}, u32[]{:S(2)}) %all-to-all-start) | async-done | bytes 8224 | tf_op jit(solution)/shard_map/all_to_all | solution.py:24
  26.2 4.6 %all-to-all-start.1 = ((bf16[128,1,1,16,320]{4,3,2,1,0:T(8,128)(2,1)}), bf16[128,1,1,16,320]{4,3,2,1,0:T(8,128)(2,1)S(1)}, u32[]{:S(2)}, u32[]{:S(2)}) async-start(bf16[128,1,1,16,320]{4,3,2,1,0:T(8,128)(2,1)} %bitcast.7), calls=%async_computation.1 | async-start | bytes 3145728 | tf_op jit(solution)/shard_map/all_to_all | solution.py:24
  30.8 0.1 eq.48
  30.9 0.1 reshape.86
  31.0 24.6 %all-to-all-done.1 = bf16[128,1,1,16,320]{4,3,2,1,0:T(8,128)(2,1)S(1)} async-done(((bf16[128,1,1,16,320]{4,3,2,1,0:T(8,128)(2,1)}), bf16[128,1,1,16,320]{4,3,2,1,0:T(8,128)(2,1)S(1)}, u32[]{:S(2)}, u32[]{:S(2)}) %all-to-all-start.1) | async-done | bytes 1310752 | tf_op jit(solution)/shard_map/all_to_all | solution.py:24
  55.6 0.0 slice-start
  55.6 0.0 copy-start.1
  55.6 0.0 slice-start.1
  55.6 7.5 %multiply_reduce_fusion = (f32[4096]{0:T(1024)S(1)}, f32[4096,320]{0,1:T(8,128)S(1)}) fusion(bf16[2048,320]{1,0:T(8,128)(2,1)S(1)} %bitcast.49, s32[2048]{0:T(1024)S(1)} %eq.48), kind=kOutput, calls=%fused_computation.9 | convolution fusion | flops 5379715072 | bytes 6578176 | tf_op jit(solution)/shard_map/dot_general | solution.py:73
  63.1 0.0 copy-done.1
  63.1 0.6 sqrt_add_fusion
  63.7 0.0 slice-done
  63.7 0.0 slice-done.1
  63.7 3.3 %divide_subtract_fusion = f32[4096,320]{0,1:T(8,128)} fusion(f32[4096,320]{0,1:T(8,128)S(1)} %bitcast.48, f32[4096,320]{0,1:T(8,128)S(1)} %get-tuple-element.6, f32[4096]{0:T(1024)S(1)} %get-tuple-element.3), kind=kLoop, calls=%fused_computation.8 | loop fusion | flops 3932160 | bytes 15745024 | tf_op jit(solution)/shard_map/sub | solution.py:75
  67.0 5.1 %copy.19 = bf16[4096,320]{1,0:T(8,128)(2,1)} copy(f32[4096,320]{0,1:T(8,128)} %divide_subtract_fusion) | data formatting | bytes 7864320 | tf_op jit(solution)/shard_map/sub | solution.py:75
  72.1 9.5 %gather_fusion = bf16[2048,320]{1,0:T(8,128)(2,1)S(1)} fusion(bf16[4096,320]{1,0:T(8,128)(2,1)} %copy.19, s32[2048]{0:T(1024)S(1)} %broadcast_clamp_fusion), kind=kCustom, calls=%fused_computation | custom fusion | bytes 2629632 | tf_op jit(solution)/shard_map/jit(_take)/gather | solution.py:76
  81.6 0.6 select_convert_fusion
  82.3 29.0 %all_to_all.15 = bf16[128,1,1,16,320]{4,3,2,1,0:T(8,128)(2,1)S(1)} all-to-all(bf16[128,1,1,16,320]{4,3,2,1,0:T(8,128)(2,1)S(1)} %select_convert_fusion), channel_id=1, replica_groups=mesh['gx'=4,'gy'=4,'gz'=8] {'gx','gy','gz'}, dimensions={0} | all-to-all | bytes 2621440 | tf_op jit(solution)/shard_map/all_to_all | solution.py:24
  111.3 2.7 %fusion.8 = bf16[1024,320]{0,1:T(8,128)(2,1)} fusion(bf16[2048,320]{1,0:T(8,128)(2,1)S(1)} %bitcast.50, s32[1024]{0:T(1024)S(1)} %convert_add_fusion), kind=kOutput, calls=%fused_computation.16 | convolution fusion | flops 1344602112 | bytes 1970176 | tf_op jit(solution)/shard_map/dot_general | solution.py:85
  (4 shorter events, 0.0 us)
Async XLA Ops:
  0.6 16.2 %copy-start = (bf16[1024,320]{0,1:T(8,128)(2,1)S(1)}, bf16[1024,320]{0,1:T(8,128)(2,1)}, u32[]{:S(2)}) copy-start(bf16[1024,320]{0,1:T(8,128)(2,1)} %param.5) | copy-start | bytes 1966084
  5.3 20.8 %all-to-all-start = ((s32[128,1,1,16]{3,2,1,0:T(1,128)}), s32[128,1,1,16]{3,2,1,0:T(1,128)S(1)}, u32[]{:S(2)}, u32[]{:S(2)}) async-start(s32[128,1,1,16]{3,2,1,0:T(1,128)} %bitcast.1), calls=%async_computation | async-start | bytes 131072 | tf_op jit(solution)/shard_map/all_to_all | solution.py:24
  26.2 29.4 %all-to-all-start.1 = ((bf16[128,1,1,16,320]{4,3,2,1,0:T(8,128)(2,1)}), bf16[128,1,1,16,320]{4,3,2,1,0:T(8,128)(2,1)S(1)}, u32[]{:S(2)}, u32[]{:S(2)}) async-start(bf16[128,1,1,16,320]{4,3,2,1,0:T(8,128)(2,1)} %bitcast.7), calls=%async_computation.1 | async-start | bytes 3145728 | tf_op jit(solution)/shard_map/all_to_all | solution.py:24
  55.6 8.1 %slice-start = ((s8[5242880]{0:T(1024)(128)(4,1)}), s8[4194304]{0:T(1024)(128)(4,1)S(1)}, s32[]{:S(2)}) async-start(s8[5242880]{0:T(1024)(128)(4,1)} %bitcast.47), calls=%async_computation.3 | async-start | bytes 8388608
  55.6 7.5 %copy-start.1 = (f32[4096]{0:T(1024)S(1)}, f32[4096]{0:T(1024)}, u32[]{:S(2)}) copy-start(f32[4096]{0:T(1024)} %param.9) | copy-start | bytes 49156
  55.6 8.1 %slice-start.1 = ((s8[5242880]{0:T(1024)(128)(4,1)}), s8[1048576]{0:T(1024)(128)(4,1)S(1)}, s32[]{:S(2)}) async-start(s8[5242880]{0:T(1024)(128)(4,1)} %bitcast.47), calls=%async_computation.4 | async-start | bytes 2097152
where the time goes:
time: 114 us
  waiting for transfers between devices  30.6 us (27%)
  blocking collectives  29 us (25%)
  local copies, waits for them, and re-layouts  17.1 us (15%)
  starting transfers between devices  16.1 us (14%)
  matrix products  13.3 us (12%)
  other arithmetic  7.1 us (6%)
    all_to_all x2, waiting for transfers between devices, joined_exchange(): lax.all_to_all(blocks, axis, split_axis=0, concat_axis=0, tiled=True)  30.6 us
    all_to_all x1, blocking collectives, joined_exchange(): lax.all_to_all(blocks, axis, split_axis=0, concat_axis=0, tiled=True)  29 us
    all_to_all x2, starting transfers between devices, joined_exchange(): lax.all_to_all(blocks, axis, split_axis=0, concat_axis=0, tiled=True)  16.1 us
    gather x1, local copies, waits for them, and re-layouts, body(): jnp.take(new_table, jnp.maximum(recv_row, 0), axis=0).astype(jnp.bfloat16)  9.49 us
    dot_general x1, matrix products, body(): grad_sum = jnp.dot(onehot, recv_grad, preferred_element_type=jnp.float32)  7.5 us
    sub x1, local copies, waits for them, and re-layouts, body(): new_table = table - 0.5 * grad_sum / (jnp.sqrt(new_accum) + 1e-08)[:, None]  5.11 us
    sub x1, other arithmetic, body(): new_table = table - 0.5 * grad_sum / (jnp.sqrt(new_accum) + 1e-08)[:, None]  3.27 us
    dot_general x1, matrix products, body(): jnp.dot(placer_bf.T, returned, preferred_element_type=jnp.float32)  2.7 us
  transfers between devices with their start and end apart: 2, of which 2 were waited for; matrix products, arithmetic and copies ran while one was open for 3% of the time, Pallas kernels for 0%

commit v1 on v0

v1 whole, which is shorter than its diff:
```python
import functools

import jax
import jax.numpy as jnp
from jax import lax
from jax.experimental import pallas as pl
from jax.experimental.pallas import tpu as pltpu
from jax.sharding import PartitionSpec as P

AXES = ("gx", "gy", "gz")
RADIX = 64
ROW_LANES = 64
LIMIT = 56 << 20


def pack_kernel(owners, cap, owner_ref, row_ref, grad_ref, send_ref, target_ref, ext_ref):
    width, tokens = grad_ref.shape
    own = owner_ref[...]
    chunk = min(256, tokens)
    first = lax.broadcasted_iota(jnp.int32, (chunk, chunk), 0)
    second = lax.broadcasted_iota(jnp.int32, (chunk, chunk), 1)
    earlier = jnp.where(first < second, 1.0, 0.0).astype(jnp.bfloat16)
    ids = lax.broadcasted_iota(jnp.int32, (owners, chunk), 0)
    seen = jnp.zeros((owners, 1), jnp.float32)
    for c in range(tokens // chunk):
        part = slice(c * chunk, (c + 1) * chunk)
        named = ids == own[:, part]
        ones = jnp.where(named, 1.0, 0.0)
        before = jnp.dot(ones.astype(jnp.bfloat16), earlier, preferred_element_type=jnp.float32)
        rank = jnp.sum(jnp.where(named, before + seen, 0.0), axis=0, keepdims=True)
        seen = seen + jnp.sum(ones, axis=1, keepdims=True)
        target_ref[:, part] = own[:, part] * cap + rank.astype(jnp.int32)
    row = row_ref[...]
    high = row // RADIX
    low = row - high * RADIX
    extra = ext_ref.shape[0] - width
    place = lax.broadcasted_iota(jnp.int32, (extra, tokens), 0)
    tail = jnp.where(place == 0, high, jnp.where(place == 1, low, 0))
    ext_ref[0:width, :] = grad_ref[...]
    ext_ref[width:, :] = tail.astype(jnp.float32).astype(jnp.bfloat16)
    target = target_ref[...]
    slots = send_ref.shape[0]
    step = min(512, slots)
    for b in range(slots // step):
        slot = lax.broadcasted_iota(jnp.int32, (step, tokens), 0) + b * step
        onehot = jnp.where(slot == target, 1.0, 0.0).astype(jnp.bfloat16)
        send_ref[b * step : (b + 1) * step, :] = lax.dot_general(
            onehot, ext_ref[...], (((1,), (1,)), ((), ())), preferred_element_type=jnp.float32
        ).astype(jnp.bfloat16)


def update_kernel(
    recv_ref, accum_ref, table_hbm, new_hbm, grown_ref, answer_ref,
    turned_ref, table_ref, new_ref, rounded_ref, in_sem, out_sem,
):
    width, rows = table_ref.shape
    slots = recv_ref.shape[0]
    tile = in_tile(rows)
    tiles = rows // tile

    def fetch(j):
        part = pl.ds(pl.multiple_of(j * tile, tile), tile)
        return pltpu.make_async_copy(table_hbm.at[:, part], table_ref.at[:, part], in_sem.at[j])

    def put(j):
        part = pl.ds(pl.multiple_of(j * tile, tile), tile)
        return pltpu.make_async_copy(new_ref.at[:, part], new_hbm.at[:, part], out_sem.at[j])

    for j in range(tiles):
        fetch(j).start()
    received = recv_ref[...]
    turned_ref[...] = received.T
    lead = received[:, width : width + 2].astype(jnp.float32).astype(jnp.int32)
    row_down = lead[:, 0:1] * RADIX + lead[:, 1:2]

    def scatter(j, carry):
        part = pl.ds(pl.multiple_of(j * tile, tile), tile)
        place = lax.broadcasted_iota(jnp.int32, (slots, tile), 1) + j * tile
        onehot = jnp.where(place == row_down, 1.0, 0.0).astype(jnp.bfloat16)
        summed = jnp.dot(turned_ref[0:width, :], onehot, preferred_element_type=jnp.float32)
        grown = accum_ref[:, part] + jnp.sum(summed * summed, axis=0, keepdims=True) / width
        grown_ref[:, part] = grown
        scale = 0.5 / (jnp.sqrt(grown) + 1e-08)
        fetch(j).wait()
        moved = table_ref[:, part] - summed * scale
        new_ref[:, part] = moved
        rounded_ref[:, part] = moved.astype(jnp.bfloat16)
        put(j).start()
        return carry

    lax.fori_loop(0, tiles, scatter, 0)
    across = turned_ref[width : width + 16, :].astype(jnp.float32).astype(jnp.int32)
    row_across = across[0:1, :] * RADIX + across[1:2, :]
    step = min(512, slots)
    for b in range(slots // step):
        place = lax.broadcasted_iota(jnp.int32, (rows, step), 0)
        onehot = jnp.where(
            place == row_across[:, b * step : (b + 1) * step], 1.0, 0.0
        ).astype(jnp.bfloat16)
        picked = jnp.dot(rounded_ref[...], onehot, preferred_element_type=jnp.float32)
        picked = picked.T.reshape(step // 16, 2, 8, width)
        lower = picked[:, 0].reshape(step // 2, width)
        upper = picked[:, 1].reshape(step // 2, width)
        answer_ref[b * step // 2 : (b + 1) * step // 2, :] = jnp.concatenate(
            [lower, upper], axis=1
        ).astype(jnp.bfloat16)
    for j in range(tiles):
        put(j).wait()


def in_tile(rows):
    return min(512, rows)


def unpack_kernel(cap, back_ref, target_ref, fresh_ref):
    width, tokens = fresh_ref.shape
    half = back_ref.shape[0]
    target = target_ref[...]
    owner = target // cap
    rank = target - owner * cap
    total = None
    for side in range(2):
        spot = jnp.where(rank // 8 == side, owner * 8 + rank - 8 * side, -1)
        place = lax.broadcasted_iota(jnp.int32, (half, tokens), 0)
        onehot = jnp.where(place == spot, 1.0, 0.0).astype(jnp.bfloat16)
        values = back_ref[:, side * width : (side + 1) * width].T
        part = jnp.dot(values, onehot, preferred_element_type=jnp.float32)
        total = part if total is None else total + part
    fresh_ref[...] = total.astype(jnp.bfloat16)


VMEM = pl.BlockSpec(memory_space=pltpu.VMEM)
ANY = pl.BlockSpec(memory_space=pl.ANY)


def pack(owner, row, grad, owners, cap):
    width, tokens = grad.shape
    wide = -(-(width + 2) // 128) * 128
    return pl.pallas_call(
        functools.partial(pack_kernel, owners, cap),
        out_shape=(
            jax.ShapeDtypeStruct((owners * cap, wide), jnp.bfloat16),
            jax.ShapeDtypeStruct((1, tokens), jnp.int32),
        ),
        in_specs=[VMEM, VMEM, VMEM],
        out_specs=(VMEM, VMEM),
        scratch_shapes=[pltpu.VMEM((wide, tokens), jnp.bfloat16)],
        compiler_params=pltpu.CompilerParams(vmem_limit_bytes=LIMIT),
        name="pack",
    )(owner, row, grad)


def update(received, accum, table):
    slots, wide = received.shape
    width, rows = table.shape
    tiles = rows // in_tile(rows)
    return pl.pallas_call(
        update_kernel,
        out_shape=(
            jax.ShapeDtypeStruct((width, rows), jnp.float32),
            jax.ShapeDtypeStruct((1, rows), jnp.float32),
            jax.ShapeDtypeStruct((slots // 2, 2 * width), jnp.bfloat16),
        ),
        in_specs=[VMEM, VMEM, ANY],
        out_specs=(ANY, VMEM, VMEM),
        scratch_shapes=[
            pltpu.VMEM((wide, slots), jnp.bfloat16),
            pltpu.VMEM((width, rows), jnp.float32),
            pltpu.VMEM((width, rows), jnp.float32),
            pltpu.VMEM((width, rows), jnp.bfloat16),
            pltpu.SemaphoreType.DMA((tiles,)),
            pltpu.SemaphoreType.DMA((tiles,)),
        ],
        compiler_params=pltpu.CompilerParams(vmem_limit_bytes=LIMIT),
        name="update",
    )(received, accum, table)


def unpack(back, target, width, cap):
    tokens = target.shape[1]
    return pl.pallas_call(
        functools.partial(unpack_kernel, cap),
        out_shape=jax.ShapeDtypeStruct((width, tokens), jnp.bfloat16),
        in_specs=[VMEM, VMEM],
        out_specs=VMEM,
        compiler_params=pltpu.CompilerParams(vmem_limit_bytes=LIMIT),
        name="unpack",
    )(back, target)


def exchange(value, devices):
    blocks = value.reshape(devices, -1, value.shape[1])
    blocks = lax.all_to_all(blocks, AXES, split_axis=0, concat_axis=0, tiled=True)
    return blocks.reshape(value.shape)


def body(token_grad, token_owner, token_row, table, accum):
    devices = lax.axis_size(AXES)
    tokens, width = token_grad.shape
    cap = 2 * tokens // devices
    send, target = pack(
        token_owner.reshape(1, tokens), token_row.reshape(1, tokens), token_grad.T, devices, cap
    )
    received = exchange(send, devices)
    new_table, new_accum, answers = update(received, accum.reshape(1, -1), table.T)
    back = exchange(answers, devices)
    fresh = unpack(back, target, width, cap)
    return (new_table.T, new_accum.reshape(-1), fresh.T)


def solution(mesh):
    split = P(AXES)
    wide = P(AXES, None)
    return jax.shard_map(
        body,
        mesh=mesh,
        in_specs=(wide, wide, split, wide, split),
        out_specs=(wide, split, wide),
        check_vma=False,
    )
```

time: 114 us -> 91.9 us (0.81)
  blocking collectives: 29 us -> 64 us
  waiting for transfers between devices: 30.6 us -> 0 us
  Pallas kernels: 0 us -> 27 us
  local copies, waits for them, and re-layouts: 17.1 us -> 0 us
  starting transfers between devices: 16.1 us -> 0 us
  matrix products: 13.3 us -> 0 us
  other arithmetic: 7.1 us -> 0 us
    all_to_all x1 -> x2, blocking collectives: 29 us -> 64 us  [exchange(): lax.all_to_all(blocks, AXES, split_axis=0, concat_axis=0, tiled=True)]
    all_to_all x2 -> x0, waiting for transfers between devices: 30.6 us -> none  [joined_exchange(): lax.all_to_all(blocks, axis, split_axis=0, concat_axis=0, tiled=True)]
    pallas_call x0 -> x3, Pallas kernels: none -> 27 us  [the longest x1 18 us: update(): pl.pallas_call(update_kernel, out_shape=(jax.ShapeDtypeStruct((width, row...]
    all_to_all x2 -> x0, starting transfers between devices: 16.1 us -> none  [joined_exchange(): lax.all_to_all(blocks, axis, split_axis=0, concat_axis=0, tiled=True)]
    dot_general x4 -> x0, matrix products: 13.3 us -> none  [the longest x1 7.5 us: body(): grad_sum = jnp.dot(onehot, recv_grad, preferred_element_type=jnp.float32)]
    gather x1 -> x0, local copies, waits for them, and re-layouts: 9.49 us -> none  [body(): jnp.take(new_table, jnp.maximum(recv_row, 0), axis=0).astype(jnp.bfloat16)]
    sub x1 -> x0, local copies, waits for them, and re-layouts: 5.11 us -> none  [body(): new_table = table - 0.5 * grad_sum / (jnp.sqrt(new_accum) + 1e-08)[:, None]]
    sub x1 -> x0, other arithmetic: 3.27 us -> none  [body(): new_table = table - 0.5 * grad_sum / (jnp.sqrt(new_accum) + 1e-08)[:, None]]
  transfers between devices with their start and end apart: 2 -> 0, of which waited for: 2 -> 0; matrix products, arithmetic and copies ran while one was open for 3% -> 0% of each run, Pallas kernels for 0% -> 0%
where the time goes in v1:
time: 91.9 us; the launch traced here: 91.6 us
  blocking collectives  64 us (70%)
  Pallas kernels  27 us (29%)
    all_to_all x2, blocking collectives, exchange(): lax.all_to_all(blocks, AXES, split_axis=0, concat_axis=0, tiled=True)  64 us
    pallas_call x1, Pallas kernels, update(): pl.pallas_call(update_kernel, out_shape=(jax.ShapeDtypeStruct((width, row...  18 us
    pallas_call x1, Pallas kernels, pack(): pl.pallas_call(functools.partial(pack_kernel, owners, cap), out_shape=(ja...  4.84 us
    pallas_call x1, Pallas kernels, unpack(): pl.pallas_call(functools.partial(unpack_kernel, cap), out_shape=jax.Shape...  4.16 us

profile of v1, /device:TPU:1, one launch (start us, length us, event | category | flops | bytes accessed | tf_op | source)
XLA Modules:
  0.0 91.6 jit_solution(18414914118575506140)
XLA Ops:
  0.6 4.8 %pack.1 = (bf16[2048,384]{1,0:T(8,128)(2,1)}, s32[1,1024]{1,0:T(1,128)}) custom-call(s32[1,1024]{1,0:T(1,128)} %bitcast.20, s32[1,1024]{1,0:T(1,128)} %bitcast.21, bf16[320,1024]{1,0:T(8,128)(2,1)} %bitcast.17), custom_call_target="tpu_custom_call" | custom-call | tf_op jit(solution)/shard_map/pack/pallas_call | solution.py:139
  5.5 36.3 %all_to_all.10 = bf16[128,16,384]{2,1,0:T(8,128)(2,1)} all-to-all(bf16[128,16,384]{2,1,0:T(8,128)(2,1)} %bitcast.15), channel_id=1, replica_groups=mesh['gx'=4,'gy'=4,'gz'=8] {'gx','gy','gz'}, dimensions={0} | all-to-all | bytes 3145728 | tf_op jit(solution)/shard_map/all_to_all | solution.py:193
  41.8 18.0 %update.1 = (f32[320,4096]{1,0:T(8,128)}, f32[1,4096]{1,0:T(1,128)}, bf16[1024,640]{1,0:T(8,128)(2,1)}) custom-call(bf16[2048,384]{1,0:T(8,128)(2,1)} %bitcast.12, f32[1,4096]{1,0:T(1,128)} %bitcast.19, f32[320,4096]{1,0:T(8,128)} %bitcast.14), custom_call_target="tpu_custom_call" | custom-call | tf_op jit(solution)/shard_map/update/pallas_call | solution.py:157
  59.8 27.7 %all_to_all.11 = bf16[128,8,640]{2,1,0:T(8,128)(2,1)} all-to-all(bf16[128,8,640]{2,1,0:T(8,128)(2,1)} %bitcast.16), channel_id=1, replica_groups=mesh['gx'=4,'gy'=4,'gz'=8] {'gx','gy','gz'}, dimensions={0} | all-to-all | bytes 2621440 | tf_op jit(solution)/shard_map/all_to_all | solution.py:193
  87.5 4.2 %unpack.1 = bf16[320,1024]{1,0:T(8,128)(2,1)} custom-call(bf16[1024,640]{1,0:T(8,128)(2,1)} %bitcast.13, s32[1,1024]{1,0:T(1,128)} %get-tuple-element.12.target_ref), custom_call_target="tpu_custom_call" | custom-call | tf_op jit(solution)/shard_map/unpack/pallas_call | solution.py:181

commit v2 on v1

--- a/solution.py
+++ b/solution.py
@@ -10,11 +10,22 @@
 AXES = ("gx", "gy", "gz")
 RADIX = 64
 ROW_LANES = 64
-LIMIT = 56 << 20
-
-
-def pack_kernel(owners, cap, owner_ref, row_ref, grad_ref, send_ref, target_ref, ext_ref):
-    width, tokens = grad_ref.shape
+LIMIT = 36 << 20
+
+
+def pack_kernel(
+    owners, cap, owner_hbm, row_hbm, grad_hbm, send_ref, target_ref,
+    ext_ref, owner_ref, row_ref, sem,
+):
+    width, tokens = grad_hbm.shape
+    owner_load = pltpu.make_async_copy(owner_hbm, owner_ref, sem.at[0])
+    row_load = pltpu.make_async_copy(row_hbm, row_ref, sem.at[1])
+    load = pltpu.make_async_copy(grad_hbm, ext_ref.at[0:width, :], sem.at[2])
+    owner_load.start()
+    row_load.start()
+    load.start()
+    owner_load.wait()
+    row_load.wait()
     own = owner_ref[...]
     chunk = min(256, tokens)
     first = lax.broadcasted_iota(jnp.int32, (chunk, chunk), 0)
@@ -36,14 +47,15 @@
     extra = ext_ref.shape[0] - width
     place = lax.broadcasted_iota(jnp.int32, (extra, tokens), 0)
     tail = jnp.where(place == 0, high, jnp.where(place == 1, low, 0))
-    ext_ref[0:width, :] = grad_ref[...]
     ext_ref[width:, :] = tail.astype(jnp.float32).astype(jnp.bfloat16)
-    target = target_ref[...]
+    load.wait()
     slots = send_ref.shape[0]
     step = min(512, slots)
+    slot = lax.broadcasted_iota(jnp.int16, (step, tokens), 0)
+    target = jnp.broadcast_to(target_ref[...], (16, tokens)).astype(jnp.int16)[0:1]
+    one, zero = jnp.bfloat16(1), jnp.bfloat16(0)
     for b in range(slots // step):
-        slot = lax.broadcasted_iota(jnp.int32, (step, tokens), 0) + b * step
-        onehot = jnp.where(slot == target, 1.0, 0.0).astype(jnp.bfloat16)
+        onehot = jnp.where(slot == target - jnp.int16(b * step), one, zero)
         send_ref[b * step : (b + 1) * step, :] = lax.dot_general(
             onehot, ext_ref[...], (((1,), (1,)), ((), ())), preferred_element_type=jnp.float32
         ).astype(jnp.bfloat16)
@@ -59,44 +71,53 @@
     tiles = rows // tile
 
     def fetch(j):
-        part = pl.ds(pl.multiple_of(j * tile, tile), tile)
+        part = pl.ds(j * tile, tile)
         return pltpu.make_async_copy(table_hbm.at[:, part], table_ref.at[:, part], in_sem.at[j])
 
     def put(j):
-        part = pl.ds(pl.multiple_of(j * tile, tile), tile)
+        part = pl.ds(j * tile, tile)
         return pltpu.make_async_copy(new_ref.at[:, part], new_hbm.at[:, part], out_sem.at[j])
 
     for j in range(tiles):
         fetch(j).start()
     received = recv_ref[...]
     turned_ref[...] = received.T
-    lead = received[:, width : width + 2].astype(jnp.float32).astype(jnp.int32)
-    row_down = lead[:, 0:1] * RADIX + lead[:, 1:2]
-
-    def scatter(j, carry):
-        part = pl.ds(pl.multiple_of(j * tile, tile), tile)
-        place = lax.broadcasted_iota(jnp.int32, (slots, tile), 1) + j * tile
-        onehot = jnp.where(place == row_down, 1.0, 0.0).astype(jnp.bfloat16)
-        summed = jnp.dot(turned_ref[0:width, :], onehot, preferred_element_type=jnp.float32)
+    across = turned_ref[width : width + 16, :].astype(jnp.float32).astype(jnp.int32)
+    row_across = across[0:1, :] * RADIX + across[1:2, :]
+    row_across = jnp.broadcast_to(row_across, (16, slots)).astype(jnp.int16)[0:1]
+    one, zero = jnp.bfloat16(1), jnp.bfloat16(0)
+
+    def summed_of(j):
+        place = lax.broadcasted_iota(jnp.int16, (tile, slots), 0)
+        onehot = jnp.where(place == row_across - jnp.int16(j * tile), one, zero)
+        return lax.dot_general(
+            turned_ref[0:width, :], onehot, (((1,), (1,)), ((), ())),
+            preferred_element_type=jnp.float32,
+        )
+
+    def settle(j, summed):
+        part = pl.ds(j * tile, tile)
         grown = accum_ref[:, part] + jnp.sum(summed * summed, axis=0, keepdims=True) / width
         grown_ref[:, part] = grown
         scale = 0.5 / (jnp.sqrt(grown) + 1e-08)
-        fetch(j).wait()
         moved = table_ref[:, part] - summed * scale
         new_ref[:, part] = moved
         rounded_ref[:, part] = moved.astype(jnp.bfloat16)
         put(j).start()
-        return carry
-
-    lax.fori_loop(0, tiles, scatter, 0)
-    across = turned_ref[width : width + 16, :].astype(jnp.float32).astype(jnp.int32)
-    row_across = across[0:1, :] * RADIX + across[1:2, :]
+
+    ahead = summed_of(0)
+    for j in range(tiles):
+        fetch(j).wait()
+    for j in range(tiles):
+        summed = ahead
+        if j + 1 < tiles:
+            ahead = summed_of(j + 1)
+        settle(j, summed)
+
     step = min(512, slots)
+    below = lax.broadcasted_iota(jnp.int16, (rows, step), 0)
     for b in range(slots // step):
-        place = lax.broadcasted_iota(jnp.int32, (rows, step), 0)
-        onehot = jnp.where(
-            place == row_across[:, b * step : (b + 1) * step], 1.0, 0.0
-        ).astype(jnp.bfloat16)
+        onehot = jnp.where(below == row_across[:, b * step : (b + 1) * step], one, zero)
         picked = jnp.dot(rounded_ref[...], onehot, preferred_element_type=jnp.float32)
         picked = picked.T.reshape(step // 16, 2, 8, width)
         lower = picked[:, 0].reshape(step // 2, width)
@@ -109,7 +130,7 @@
 
 
 def in_tile(rows):
-    return min(512, rows)
+    return min(1024, rows)
 
 
 def unpack_kernel(cap, back_ref, target_ref, fresh_ref):
@@ -121,8 +142,9 @@
     total = None
     for side in range(2):
         spot = jnp.where(rank // 8 == side, owner * 8 + rank - 8 * side, -1)
-        place = lax.broadcasted_iota(jnp.int32, (half, tokens), 0)
-        onehot = jnp.where(place == spot, 1.0, 0.0).astype(jnp.bfloat16)
+        spot = jnp.broadcast_to(spot, (16, tokens)).astype(jnp.int16)[0:1]
+        place = lax.broadcasted_iota(jnp.int16, (half, tokens), 0)
+        onehot = jnp.where(place == spot, jnp.bfloat16(1), jnp.bfloat16(0))
         values = back_ref[:, side * width : (side + 1) * width].T
         part = jnp.dot(values, onehot, preferred_element_type=jnp.float32)
         total = part if total is None else total + part
@@ -130,7 +152,7 @@
 
 
 VMEM = pl.BlockSpec(memory_space=pltpu.VMEM)
-ANY = pl.BlockSpec(memory_space=pl.ANY)
+HBM = pl.BlockSpec(memory_space=pltpu.HBM)
 
 
 def pack(owner, row, grad, owners, cap):
@@ -142,12 +164,17 @@
             jax.ShapeDtypeStruct((owners * cap, wide), jnp.bfloat16),
             jax.ShapeDtypeStruct((1, tokens), jnp.int32),
         ),
-        in_specs=[VMEM, VMEM, VMEM],
+        in_specs=[HBM, HBM, HBM],
         out_specs=(VMEM, VMEM),
-        scratch_shapes=[pltpu.VMEM((wide, tokens), jnp.bfloat16)],
+        scratch_shapes=[
+            pltpu.VMEM((wide, tokens), jnp.bfloat16),
+            pltpu.VMEM((1, tokens), jnp.int32),
+            pltpu.VMEM((1, tokens), jnp.int32),
+            pltpu.SemaphoreType.DMA((3,)),
+        ],
         compiler_params=pltpu.CompilerParams(vmem_limit_bytes=LIMIT),
         name="pack",
-    )(owner, row, grad)
+    )(*(pltpu.with_memory_space_constraint(x, pltpu.HBM) for x in (owner, row, grad)))
 
 
 def update(received, accum, table):
@@ -161,8 +188,8 @@
             jax.ShapeDtypeStruct((1, rows), jnp.float32),
             jax.ShapeDtypeStruct((slots // 2, 2 * width), jnp.bfloat16),
         ),
-        in_specs=[VMEM, VMEM, ANY],
-        out_specs=(ANY, VMEM, VMEM),
+        in_specs=[VMEM, VMEM, HBM],
+        out_specs=(HBM, VMEM, VMEM),
         scratch_shapes=[
             pltpu.VMEM((wide, slots), jnp.bfloat16),
             pltpu.VMEM((width, rows), jnp.float32),
@@ -173,7 +200,7 @@
         ],
         compiler_params=pltpu.CompilerParams(vmem_limit_bytes=LIMIT),
         name="update",
-    )(received, accum, table)
+    )(received, accum, pltpu.with_memory_space_constraint(table, pltpu.HBM))
 
 
 def unpack(back, target, width, cap):

time: 91.9 us -> 83.8 us (0.912)
  Pallas kernels: 27 us -> 20.8 us
  blocking collectives: 64 us -> 62.1 us
    pallas_call x1, Pallas kernels: 18 us -> 14.5 us  [update(): pl.pallas_call(update_kernel, out_shape=(jax.ShapeDtypeStruct((width, row...]
    all_to_all x2, blocking collectives: 64 us -> 62.1 us  [exchange(): lax.all_to_all(blocks, AXES, split_axis=0, concat_axis=0, tiled=True)]
    pallas_call x1, Pallas kernels: 4.16 us -> 2.78 us  [unpack(): pl.pallas_call(functools.partial(unpack_kernel, cap), out_shape=jax.Shape...]
    pallas_call x1, Pallas kernels: 4.84 us -> 3.49 us  [pack(): pl.pallas_call(functools.partial(pack_kernel, owners, cap), out_shape=(ja...]
where the time goes in v2:
time: 83.8 us; the launch traced here: 83.5 us
  blocking collectives  62.1 us (74%)
  Pallas kernels  20.8 us (25%)
    all_to_all x2, blocking collectives, exchange(): lax.all_to_all(blocks, AXES, split_axis=0, concat_axis=0, tiled=True)  62.1 us
    pallas_call x1, Pallas kernels, update(): pl.pallas_call(update_kernel, out_shape=(jax.ShapeDtypeStruct((width, row...  14.5 us
    pallas_call x1, Pallas kernels, pack(): pl.pallas_call(functools.partial(pack_kernel, owners, cap), out_shape=(ja...  3.49 us
    pallas_call x1, Pallas kernels, unpack(): pl.pallas_call(functools.partial(unpack_kernel, cap), out_shape=jax.Shape...  2.78 us

profile of v2, /device:TPU:1, one launch (start us, length us, event | category | flops | bytes accessed | tf_op | source)
XLA Modules:
  0.0 83.5 jit_solution(3008906450569920676)
XLA Ops:
  0.6 3.5 %pack.1 = (bf16[2048,384]{1,0:T(8,128)(2,1)S(1)}, s32[1,1024]{1,0:T(1,128)S(1)}) custom-call(s32[1,1024]{1,0:T(1,128)} %bitcast.20, s32[1,1024]{1,0:T(1,128)} %bitcast.21, bf16[320,1024]{1,0:T(8,128)(2,1)} %bitcast.18), custom_call_target="tpu_custom_call" | custom-call | tf_op jit(solution)/shard_map/pack/pallas_call | solution.py:161
  4.1 0.0 copy-start
  4.1 36.0 %all_to_all.10 = bf16[128,16,384]{2,1,0:T(8,128)(2,1)S(1)} all-to-all(bf16[128,16,384]{2,1,0:T(8,128)(2,1)S(1)} %bitcast.14), channel_id=1, replica_groups=mesh['gx'=4,'gy'=4,'gz'=8] {'gx','gy','gz'}, dimensions={0} | all-to-all | bytes 3145728 | tf_op jit(solution)/shard_map/all_to_all | solution.py:220
  40.1 0.0 copy-done
  40.1 14.5 %update.1 = (f32[320,4096]{1,0:T(8,128)}, f32[1,4096]{1,0:T(1,128)}, bf16[1024,640]{1,0:T(8,128)(2,1)S(1)}) custom-call(bf16[2048,384]{1,0:T(8,128)(2,1)S(1)} %bitcast.12, f32[1,4096]{1,0:T(1,128)S(1)} %bitcast.16, f32[320,4096]{1,0:T(8,128)} %bitcast.17), custom_call_target="tpu_custom_call" | custom-call | tf_op jit(solution)/shard_map/update/pallas_call | solution.py:184
  54.7 26.1 %all_to_all.11 = bf16[128,8,640]{2,1,0:T(8,128)(2,1)S(1)} all-to-all(bf16[128,8,640]{2,1,0:T(8,128)(2,1)S(1)} %bitcast.15), channel_id=1, replica_groups=mesh['gx'=4,'gy'=4,'gz'=8] {'gx','gy','gz'}, dimensions={0} | all-to-all | bytes 2621440 | tf_op jit(solution)/shard_map/all_to_all | solution.py:220
  80.8 2.8 %unpack.1 = bf16[320,1024]{1,0:T(8,128)(2,1)} custom-call(bf16[1024,640]{1,0:T(8,128)(2,1)S(1)} %bitcast.13, s32[1,1024]{1,0:T(1,128)S(1)} %get-tuple-element.12.target_ref), custom_call_target="tpu_custom_call" | custom-call | tf_op jit(solution)/shard_map/unpack/pallas_call | solution.py:208
Async XLA Ops:
  4.1 36.0 %copy-start = (f32[4096]{0:T(1024)S(1)}, f32[4096]{0:T(1024)}, u32[]{:S(2)}) copy-start(f32[4096]{0:T(1024)} %param.9) | copy-start | bytes 49156

commit v3 on v2

--- a/solution.py
+++ b/solution.py
@@ -50,15 +50,18 @@
     ext_ref[width:, :] = tail.astype(jnp.float32).astype(jnp.bfloat16)
     load.wait()
     slots = send_ref.shape[0]
+    wide = width + 16
     step = min(512, slots)
     slot = lax.broadcasted_iota(jnp.int16, (step, tokens), 0)
     target = jnp.broadcast_to(target_ref[...], (16, tokens)).astype(jnp.int16)[0:1]
     one, zero = jnp.bfloat16(1), jnp.bfloat16(0)
     for b in range(slots // step):
         onehot = jnp.where(slot == target - jnp.int16(b * step), one, zero)
-        send_ref[b * step : (b + 1) * step, :] = lax.dot_general(
-            onehot, ext_ref[...], (((1,), (1,)), ((), ())), preferred_element_type=jnp.float32
+        placed = lax.dot_general(
+            ext_ref[0:wide, :], onehot, (((1,), (1,)), ((), ())),
+            preferred_element_type=jnp.float32,
         ).astype(jnp.bfloat16)
+        send_ref[b * step : (b + 1) * step, 0:wide] = placed.T
 
 
 def update_kernel(
@@ -103,16 +106,18 @@
         moved = table_ref[:, part] - summed * scale
         new_ref[:, part] = moved
         rounded_ref[:, part] = moved.astype(jnp.bfloat16)
-        put(j).start()
 
     ahead = summed_of(0)
-    for j in range(tiles):
-        fetch(j).wait()
     for j in range(tiles):
         summed = ahead
         if j + 1 < tiles:
             ahead = summed_of(j + 1)
+        if j == 0:
+            for i in range(tiles):
+                fetch(i).wait()
         settle(j, summed)
+    for j in range(tiles):
+        put(j).start()
 
     step = min(512, slots)
     below = lax.broadcasted_iota(jnp.int16, (rows, step), 0)
@@ -130,25 +135,35 @@
 
 
 def in_tile(rows):
-    return min(1024, rows)
-
-
-def unpack_kernel(cap, back_ref, target_ref, fresh_ref):
-    width, tokens = fresh_ref.shape
+    return min(2048, rows)
+
+
+def unpack_kernel(cap, back_ref, target_ref, fresh_hbm, turned_ref, fresh_ref, sem):
+    width, tokens = fresh_hbm.shape
     half = back_ref.shape[0]
     target = target_ref[...]
     owner = target // cap
     rank = target - owner * cap
-    total = None
-    for side in range(2):
-        spot = jnp.where(rank // 8 == side, owner * 8 + rank - 8 * side, -1)
-        spot = jnp.broadcast_to(spot, (16, tokens)).astype(jnp.int16)[0:1]
-        place = lax.broadcasted_iota(jnp.int16, (half, tokens), 0)
-        onehot = jnp.where(place == spot, jnp.bfloat16(1), jnp.bfloat16(0))
-        values = back_ref[:, side * width : (side + 1) * width].T
-        part = jnp.dot(values, onehot, preferred_element_type=jnp.float32)
-        total = part if total is None else total + part
-    fresh_ref[...] = total.astype(jnp.bfloat16)
+    side = rank // 8
+    spot = side * half + owner * 8 + rank - 8 * side
+    spot = jnp.broadcast_to(spot, (16, tokens)).astype(jnp.int16)[0:1]
+    turned = back_ref[...].T
+    turned_ref[:, 0:half] = turned[0:width]
+    turned_ref[:, half:] = turned[width:]
+    step = tokens // 2
+    place = lax.broadcasted_iota(jnp.int16, (2 * half, step), 0)
+    copies = []
+    for b in range(2):
+        part = slice(b * step, (b + 1) * step)
+        onehot = jnp.where(place == spot[:, part], jnp.bfloat16(1), jnp.bfloat16(0))
+        fresh_ref[:, part] = jnp.dot(
+            turned_ref[...], onehot, preferred_element_type=jnp.float32
+        ).astype(jnp.bfloat16)
+        copy = pltpu.make_async_copy(fresh_ref.at[:, part], fresh_hbm.at[:, part], sem.at[b])
+        copy.start()
+        copies.append(copy)
+    for copy in copies:
+        copy.wait()
 
 
 VMEM = pl.BlockSpec(memory_space=pltpu.VMEM)
@@ -209,7 +224,12 @@
         functools.partial(unpack_kernel, cap),
         out_shape=jax.ShapeDtypeStruct((width, tokens), jnp.bfloat16),
         in_specs=[VMEM, VMEM],
-        out_specs=VMEM,
+        out_specs=HBM,
+        scratch_shapes=[
+            pltpu.VMEM((width, 2 * back.shape[0]), jnp.bfloat16),
+            pltpu.VMEM((width, tokens), jnp.bfloat16),
+            pltpu.SemaphoreType.DMA((2,)),
+        ],
         compiler_params=pltpu.CompilerParams(vmem_limit_bytes=LIMIT),
         name="unpack",
     )(back, target)

time: 83.8 us -> 80.8 us (0.964)
  Pallas kernels: 20.8 us -> 17.8 us
    pallas_call x1, Pallas kernels: 14.5 us -> 12.7 us  [update(): pl.pallas_call(update_kernel, out_shape=(jax.ShapeDtypeStruct((width, row...]
where the time goes in v3:
time: 80.8 us; the launch traced here: 80.6 us
  blocking collectives  62.1 us (77%)
  Pallas kernels  17.8 us (22%)
    all_to_all x2, blocking collectives, exchange(): lax.all_to_all(blocks, AXES, split_axis=0, concat_axis=0, tiled=True)  62.1 us
    pallas_call x1, Pallas kernels, update(): pl.pallas_call(update_kernel, out_shape=(jax.ShapeDtypeStruct((width, row...  12.7 us
    pallas_call x1, Pallas kernels, pack(): pl.pallas_call(functools.partial(pack_kernel, owners, cap), out_shape=(ja...  2.86 us
    pallas_call x1, Pallas kernels, unpack(): pl.pallas_call(functools.partial(unpack_kernel, cap), out_shape=jax.Shape...  2.3 us

profile of v3, /device:TPU:1, one launch (start us, length us, event | category | flops | bytes accessed | tf_op | source)
XLA Modules:
  0.0 80.6 jit_solution(12364147664321033690)
XLA Ops:
  0.6 2.9 %pack.1 = (bf16[2048,384]{1,0:T(8,128)(2,1)S(1)}, s32[1,1024]{1,0:T(1,128)S(1)}) custom-call(s32[1,1024]{1,0:T(1,128)} %bitcast.20, s32[1,1024]{1,0:T(1,128)} %bitcast.21, bf16[320,1024]{1,0:T(8,128)(2,1)} %bitcast.18), custom_call_target="tpu_custom_call" | custom-call | tf_op jit(solution)/shard_map/pack/pallas_call | solution.py:176
  3.5 0.0 copy-start
  3.5 36.0 %all_to_all.10 = bf16[128,16,384]{2,1,0:T(8,128)(2,1)S(1)} all-to-all(bf16[128,16,384]{2,1,0:T(8,128)(2,1)S(1)} %bitcast.14), channel_id=1, replica_groups=mesh['gx'=4,'gy'=4,'gz'=8] {'gx','gy','gz'}, dimensions={0} | all-to-all | bytes 3145728 | tf_op jit(solution)/shard_map/all_to_all | solution.py:240
  39.5 0.0 copy-done
  39.5 12.7 %update.1 = (f32[320,4096]{1,0:T(8,128)}, f32[1,4096]{1,0:T(1,128)}, bf16[1024,640]{1,0:T(8,128)(2,1)S(1)}) custom-call(bf16[2048,384]{1,0:T(8,128)(2,1)S(1)} %bitcast.12, f32[1,4096]{1,0:T(1,128)S(1)} %bitcast.16, f32[320,4096]{1,0:T(8,128)} %bitcast.17), custom_call_target="tpu_custom_call" | custom-call | tf_op jit(solution)/shard_map/update/pallas_call | solution.py:199
  52.2 26.1 %all_to_all.11 = bf16[128,8,640]{2,1,0:T(8,128)(2,1)S(1)} all-to-all(bf16[128,8,640]{2,1,0:T(8,128)(2,1)S(1)} %bitcast.15), channel_id=1, replica_groups=mesh['gx'=4,'gy'=4,'gz'=8] {'gx','gy','gz'}, dimensions={0} | all-to-all | bytes 2621440 | tf_op jit(solution)/shard_map/all_to_all | solution.py:240
  78.3 2.3 %unpack.1 = bf16[320,1024]{1,0:T(8,128)(2,1)} custom-call(bf16[1024,640]{1,0:T(8,128)(2,1)S(1)} %bitcast.13, s32[1,1024]{1,0:T(1,128)S(1)} %get-tuple-element.12.target_ref), custom_call_target="tpu_custom_call" | custom-call | tf_op jit(solution)/shard_map/unpack/pallas_call | solution.py:223
Async XLA Ops:
  3.5 36.0 %copy-start = (f32[4096]{0:T(1024)S(1)}, f32[4096]{0:T(1024)}, u32[]{:S(2)}) copy-start(f32[4096]{0:T(1024)} %param.9) | copy-start | bytes 49156

commit v4 on v3

--- a/solution.py
+++ b/solution.py
@@ -64,27 +64,24 @@
         send_ref[b * step : (b + 1) * step, 0:wide] = placed.T
 
 
+def copies_of(source, target, sem):
+    count = sem.shape[0]
+    piece = source.shape[1] // count
+    parts = [slice(i * piece, (i + 1) * piece) for i in range(count)]
+    return [
+        pltpu.make_async_copy(source.at[:, part], target.at[:, part], sem.at[i])
+        for i, part in enumerate(parts)
+    ]
+
+
 def update_kernel(
-    recv_ref, accum_ref, table_hbm, new_hbm, grown_ref, answer_ref,
-    turned_ref, table_ref, new_ref, rounded_ref, in_sem, out_sem,
+    recv_ref, accum_ref, table_ref, new_ref, grown_ref, answer_ref, turned_ref, rounded_ref
 ):
     width, rows = table_ref.shape
     slots = recv_ref.shape[0]
     tile = in_tile(rows)
     tiles = rows // tile
-
-    def fetch(j):
-        part = pl.ds(j * tile, tile)
-        return pltpu.make_async_copy(table_hbm.at[:, part], table_ref.at[:, part], in_sem.at[j])
-
-    def put(j):
-        part = pl.ds(j * tile, tile)
-        return pltpu.make_async_copy(new_ref.at[:, part], new_hbm.at[:, part], out_sem.at[j])
-
-    for j in range(tiles):
-        fetch(j).start()
-    received = recv_ref[...]
-    turned_ref[...] = received.T
+    turned_ref[...] = recv_ref[...].T
     across = turned_ref[width : width + 16, :].astype(jnp.float32).astype(jnp.int32)
     row_across = across[0:1, :] * RADIX + across[1:2, :]
     row_across = jnp.broadcast_to(row_across, (16, slots)).astype(jnp.int16)[0:1]
@@ -112,12 +109,7 @@
         summed = ahead
         if j + 1 < tiles:
             ahead = summed_of(j + 1)
-        if j == 0:
-            for i in range(tiles):
-                fetch(i).wait()
         settle(j, summed)
-    for j in range(tiles):
-        put(j).start()
 
     step = min(512, slots)
     below = lax.broadcasted_iota(jnp.int16, (rows, step), 0)
@@ -130,15 +122,18 @@
         answer_ref[b * step // 2 : (b + 1) * step // 2, :] = jnp.concatenate(
             [lower, upper], axis=1
         ).astype(jnp.bfloat16)
-    for j in range(tiles):
-        put(j).wait()
 
 
 def in_tile(rows):
     return min(2048, rows)
 
 
-def unpack_kernel(cap, back_ref, target_ref, fresh_hbm, turned_ref, fresh_ref, sem):
+def unpack_kernel(
+    cap, back_ref, target_ref, table_ref, fresh_hbm, table_hbm, turned_ref, fresh_ref, sem, table_sem
+):
+    copies = copies_of(table_ref, table_hbm, table_sem)
+    for copy in copies:
+        copy.start()
     width, tokens = fresh_hbm.shape
     half = back_ref.shape[0]
     target = target_ref[...]
@@ -152,7 +147,6 @@
     turned_ref[:, half:] = turned[width:]
     step = tokens // 2
     place = lax.broadcasted_iota(jnp.int16, (2 * half, step), 0)
-    copies = []
     for b in range(2):
         part = slice(b * step, (b + 1) * step)
         onehot = jnp.where(place == spot[:, part], jnp.bfloat16(1), jnp.bfloat16(0))
@@ -166,6 +160,13 @@
         copy.wait()
 
 
+def cost(depth, rows, columns, *arrays):
+    moved = sum(x.size * x.dtype.itemsize for x in arrays)
+    return pl.CostEstimate(
+        flops=2 * depth * rows * columns, transcendentals=0, bytes_accessed=moved
+    )
+
+
 VMEM = pl.BlockSpec(memory_space=pltpu.VMEM)
 HBM = pl.BlockSpec(memory_space=pltpu.HBM)
 
@@ -173,10 +174,11 @@
 def pack(owner, row, grad, owners, cap):
     width, tokens = grad.shape
     wide = -(-(width + 2) // 128) * 128
+    sent = jax.ShapeDtypeStruct((owners * cap, wide), jnp.bfloat16)
     return pl.pallas_call(
         functools.partial(pack_kernel, owners, cap),
         out_shape=(
-            jax.ShapeDtypeStruct((owners * cap, wide), jnp.bfloat16),
+            sent,
             jax.ShapeDtypeStruct((1, tokens), jnp.int32),
         ),
         in_specs=[HBM, HBM, HBM],
@@ -188,6 +190,7 @@
             pltpu.SemaphoreType.DMA((3,)),
         ],
         compiler_params=pltpu.CompilerParams(vmem_limit_bytes=LIMIT),
+        cost_estimate=cost(tokens, owners * cap, wide, owner, row, grad, sent),
         name="pack",
     )(*(pltpu.with_memory_space_constraint(x, pltpu.HBM) for x in (owner, row, grad)))
 
@@ -195,7 +198,6 @@
 def update(received, accum, table):
     slots, wide = received.shape
     width, rows = table.shape
-    tiles = rows // in_tile(rows)
     return pl.pallas_call(
         update_kernel,
         out_shape=(
@@ -203,36 +205,39 @@
             jax.ShapeDtypeStruct((1, rows), jnp.float32),
             jax.ShapeDtypeStruct((slots // 2, 2 * width), jnp.bfloat16),
         ),
-        in_specs=[VMEM, VMEM, HBM],
-        out_specs=(HBM, VMEM, VMEM),
+        in_specs=[VMEM, VMEM, VMEM],
+        out_specs=(VMEM, VMEM, VMEM),
         scratch_shapes=[
             pltpu.VMEM((wide, slots), jnp.bfloat16),
-            pltpu.VMEM((width, rows), jnp.float32),
-            pltpu.VMEM((width, rows), jnp.float32),
             pltpu.VMEM((width, rows), jnp.bfloat16),
-            pltpu.SemaphoreType.DMA((tiles,)),
-            pltpu.SemaphoreType.DMA((tiles,)),
         ],
         compiler_params=pltpu.CompilerParams(vmem_limit_bytes=LIMIT),
+        cost_estimate=cost(2 * slots, rows, width, received, accum, table, table),
         name="update",
-    )(received, accum, pltpu.with_memory_space_constraint(table, pltpu.HBM))
-
-
-def unpack(back, target, width, cap):
+    )(received, accum, table)
+
+
+def unpack(back, target, table, cap):
     tokens = target.shape[1]
+    width = table.shape[0]
     return pl.pallas_call(
         functools.partial(unpack_kernel, cap),
-        out_shape=jax.ShapeDtypeStruct((width, tokens), jnp.bfloat16),
-        in_specs=[VMEM, VMEM],
-        out_specs=HBM,
+        out_shape=(
+            jax.ShapeDtypeStruct((width, tokens), jnp.bfloat16),
+            jax.ShapeDtypeStruct(table.shape, jnp.float32),
+        ),
+        in_specs=[VMEM, VMEM, VMEM],
+        out_specs=(HBM, HBM),
         scratch_shapes=[
             pltpu.VMEM((width, 2 * back.shape[0]), jnp.bfloat16),
             pltpu.VMEM((width, tokens), jnp.bfloat16),
             pltpu.SemaphoreType.DMA((2,)),
+            pltpu.SemaphoreType.DMA((4,)),
         ],
         compiler_params=pltpu.CompilerParams(vmem_limit_bytes=LIMIT),
+        cost_estimate=cost(2 * back.shape[0], width, tokens, back, table),
         name="unpack",
-    )(back, target)
+    )(back, target, table)
 
 
 def exchange(value, devices):
@@ -249,9 +254,9 @@
         token_owner.reshape(1, tokens), token_row.reshape(1, tokens), token_grad.T, devices, cap
     )
     received = exchange(send, devices)
-    new_table, new_accum, answers = update(received, accum.reshape(1, -1), table.T)
+    updated, new_accum, answers = update(received, accum.reshape(1, -1), table.T)
     back = exchange(answers, devices)
-    fresh = unpack(back, target, width, cap)
+    fresh, new_table = unpack(back, target, updated, cap)
     return (new_table.T, new_accum.reshape(-1), fresh.T)
 
 

time: 80.8 us -> 80.2 us (level)
    pallas_call x1, Pallas kernels: 12.7 us -> 11.7 us  [update(): pl.pallas_call(update_kernel, out_shape=(jax.ShapeDtypeStruct((width, row...]
where the time goes in v4:
time: 80.2 us; the launch traced here: 80 us
  blocking collectives  62.1 us (77%)
  Pallas kernels  17.3 us (22%)
    all_to_all x2, blocking collectives, exchange(): lax.all_to_all(blocks, AXES, split_axis=0, concat_axis=0, tiled=True)  62.1 us
    pallas_call x1, Pallas kernels, update(): pl.pallas_call(update_kernel, out_shape=(jax.ShapeDtypeStruct((width, row...  11.7 us
    pallas_call x1, Pallas kernels, pack(): pl.pallas_call(functools.partial(pack_kernel, owners, cap), out_shape=(se...  3.01 us
    pallas_call x1, Pallas kernels, unpack(): pl.pallas_call(functools.partial(unpack_kernel, cap), out_shape=(jax.Shap...  2.58 us

profile of v4, /device:TPU:1, one launch (start us, length us, event | category | flops | bytes accessed | tf_op | source)
XLA Modules:
  0.0 80.0 jit_solution(7843145103605296184)
XLA Ops:
  0.6 0.0 copy-start
  0.6 3.0 %pack.1 = (bf16[2048,384]{1,0:T(8,128)(2,1)S(1)}, s32[1,1024]{1,0:T(1,128)S(1)}) custom-call(s32[1,1024]{1,0:T(1,128)} %bitcast.21, s32[1,1024]{1,0:T(1,128)} %bitcast.22, bf16[320,1024]{1,0:T(8,128)(2,1)} %bitcast.19), custom_call_target="tpu_custom_call" | custom-call | flops 1610612736 | bytes 2236416 | tf_op jit(solution)/shard_map/pack/pallas_call | solution.py:178
  3.7 0.0 copy-start.1
  3.7 36.0 %all_to_all.10 = bf16[128,16,384]{2,1,0:T(8,128)(2,1)S(1)} all-to-all(bf16[128,16,384]{2,1,0:T(8,128)(2,1)S(1)} %bitcast.14), channel_id=1, replica_groups=mesh['gx'=4,'gy'=4,'gz'=8] {'gx','gy','gz'}, dimensions={0} | all-to-all | bytes 3145728 | tf_op jit(solution)/shard_map/all_to_all | solution.py:245
  39.7 0.0 copy-done
  39.7 0.0 copy-done.1
  39.7 11.7 %update.1 = (f32[320,4096]{1,0:T(8,128)S(1)}, f32[1,4096]{1,0:T(1,128)}, bf16[1024,640]{1,0:T(8,128)(2,1)S(1)}) custom-call(bf16[2048,384]{1,0:T(8,128)(2,1)S(1)} %bitcast.13, f32[1,4096]{1,0:T(1,128)S(1)} %bitcast.17, f32[320,4096]{1,0:T(8,128)S(1)} %bitcast.16), custom_call_target="tpu_custom_call" | custom-call | flops 10737418240 | bytes 12075008 | tf_op jit(solution)/shard_map/update/pallas_call | solution.py:201
  51.4 26.1 %all_to_all.11 = bf16[128,8,640]{2,1,0:T(8,128)(2,1)S(1)} all-to-all(bf16[128,8,640]{2,1,0:T(8,128)(2,1)S(1)} %bitcast.15), channel_id=1, replica_groups=mesh['gx'=4,'gy'=4,'gz'=8] {'gx','gy','gz'}, dimensions={0} | all-to-all | bytes 2621440 | tf_op jit(solution)/shard_map/all_to_all | solution.py:245
  77.4 2.6 %unpack.1 = (bf16[320,1024]{1,0:T(8,128)(2,1)}, f32[320,4096]{1,0:T(8,128)}) custom-call(bf16[1024,640]{1,0:T(8,128)(2,1)S(1)} %bitcast.12, s32[1,1024]{1,0:T(1,128)S(1)} %get-tuple-element.12.target_ref, f32[320,4096]{1,0:T(8,128)S(1)} %get-tuple-element.13.table_ref), custom_call_target="tpu_custom_call" | custom-call | flops 1342177280 | bytes 6553600 | tf_op jit(solution)/shard_map/unpack/pallas_call | solution.py:223
Async XLA Ops:
  0.6 39.0 %copy-start = (f32[4096,320]{0,1:T(8,128)S(1)}, f32[4096,320]{0,1:T(8,128)}, u32[]{:S(2)}) copy-start(f32[4096,320]{0,1:T(8,128)} %param.8) | copy-start | bytes 15728644
  3.7 36.0 %copy-start.1 = (f32[4096]{0:T(1024)S(1)}, f32[4096]{0:T(1024)}, u32[]{:S(2)}) copy-start(f32[4096]{0:T(1024)} %param.9) | copy-start | bytes 49156

commit v5 on v4

--- a/solution.py
+++ b/solution.py
@@ -75,7 +75,8 @@
 
 
 def update_kernel(
-    recv_ref, accum_ref, table_ref, new_ref, grown_ref, answer_ref, turned_ref, rounded_ref
+    recv_ref, accum_ref, table_ref, new_hbm, rest_ref, grown_hbm, answer_ref,
+    turned_ref, rounded_ref, grown_ref, sem, new_ref, new_sem,
 ):
     width, rows = table_ref.shape
     slots = recv_ref.shape[0]
@@ -101,7 +102,10 @@
         grown_ref[:, part] = grown
         scale = 0.5 / (jnp.sqrt(grown) + 1e-08)
         moved = table_ref[:, part] - summed * scale
-        new_ref[:, part] = moved
+        if j + 1 < tiles:
+            new_ref[:, part] = moved
+        else:
+            rest_ref[...] = moved
         rounded_ref[:, part] = moved.astype(jnp.bfloat16)
 
     ahead = summed_of(0)
@@ -110,6 +114,12 @@
         if j + 1 < tiles:
             ahead = summed_of(j + 1)
         settle(j, summed)
+    grown_copy = pltpu.make_async_copy(grown_ref, grown_hbm, sem)
+    grown_copy.start()
+    early = rows - tile
+    copies = copies_of(new_ref, new_hbm.at[:, 0:early], new_sem)
+    for copy in copies:
+        copy.start()
 
     step = min(512, slots)
     below = lax.broadcasted_iota(jnp.int16, (rows, step), 0)
@@ -122,6 +132,9 @@
         answer_ref[b * step // 2 : (b + 1) * step // 2, :] = jnp.concatenate(
             [lower, upper], axis=1
         ).astype(jnp.bfloat16)
+    grown_copy.wait()
+    for copy in copies:
+        copy.wait()
 
 
 def in_tile(rows):
@@ -129,9 +142,10 @@
 
 
 def unpack_kernel(
-    cap, back_ref, target_ref, table_ref, fresh_hbm, table_hbm, turned_ref, fresh_ref, sem, table_sem
+    cap, back_ref, target_ref, rest_ref, part_hbm, fresh_hbm, table_hbm, turned_ref, fresh_ref, sem, table_sem
 ):
-    copies = copies_of(table_ref, table_hbm, table_sem)
+    rows, tile = table_hbm.shape[1], rest_ref.shape[1]
+    copies = copies_of(rest_ref, table_hbm.at[:, rows - tile : rows], table_sem)
     for copy in copies:
         copy.start()
     width, tokens = fresh_hbm.shape
@@ -198,18 +212,24 @@
 def update(received, accum, table):
     slots, wide = received.shape
     width, rows = table.shape
+    tile = in_tile(rows)
     return pl.pallas_call(
         update_kernel,
         out_shape=(
             jax.ShapeDtypeStruct((width, rows), jnp.float32),
+            jax.ShapeDtypeStruct((width, tile), jnp.float32),
             jax.ShapeDtypeStruct((1, rows), jnp.float32),
             jax.ShapeDtypeStruct((slots // 2, 2 * width), jnp.bfloat16),
         ),
         in_specs=[VMEM, VMEM, VMEM],
-        out_specs=(VMEM, VMEM, VMEM),
+        out_specs=(HBM, VMEM, HBM, VMEM),
         scratch_shapes=[
             pltpu.VMEM((wide, slots), jnp.bfloat16),
             pltpu.VMEM((width, rows), jnp.bfloat16),
+            pltpu.VMEM((1, rows), jnp.float32),
+            pltpu.SemaphoreType.DMA,
+            pltpu.VMEM((width, rows - tile), jnp.float32),
+            pltpu.SemaphoreType.DMA((2,)),
         ],
         compiler_params=pltpu.CompilerParams(vmem_limit_bytes=LIMIT),
         cost_estimate=cost(2 * slots, rows, width, received, accum, table, table),
@@ -217,7 +237,7 @@
     )(received, accum, table)
 
 
-def unpack(back, target, table, cap):
+def unpack(back, target, rest, table, cap):
     tokens = target.shape[1]
     width = table.shape[0]
     return pl.pallas_call(
@@ -226,8 +246,9 @@
             jax.ShapeDtypeStruct((width, tokens), jnp.bfloat16),
             jax.ShapeDtypeStruct(table.shape, jnp.float32),
         ),
-        in_specs=[VMEM, VMEM, VMEM],
+        in_specs=[VMEM, VMEM, VMEM, HBM],
         out_specs=(HBM, HBM),
+        input_output_aliases={3: 1},
         scratch_shapes=[
             pltpu.VMEM((width, 2 * back.shape[0]), jnp.bfloat16),
             pltpu.VMEM((width, tokens), jnp.bfloat16),
@@ -237,7 +258,7 @@
         compiler_params=pltpu.CompilerParams(vmem_limit_bytes=LIMIT),
         cost_estimate=cost(2 * back.shape[0], width, tokens, back, table),
         name="unpack",
-    )(back, target, table)
+    )(back, target, rest, table)
 
 
 def exchange(value, devices):
@@ -254,9 +275,9 @@
         token_owner.reshape(1, tokens), token_row.reshape(1, tokens), token_grad.T, devices, cap
     )
     received = exchange(send, devices)
-    updated, new_accum, answers = update(received, accum.reshape(1, -1), table.T)
+    early, rest, new_accum, answers = update(received, accum.reshape(1, -1), table.T)
     back = exchange(answers, devices)
-    fresh, new_table = unpack(back, target, updated, cap)
+    fresh, new_table = unpack(back, target, rest, early, cap)
     return (new_table.T, new_accum.reshape(-1), fresh.T)
 
 

time: 80.2 us -> 80 us (level)
  no operation moved by 1% of the time
where the time goes in v5:
time: 80 us; the launch traced here: 79.8 us
  blocking collectives  62.1 us (78%)
  Pallas kernels  17 us (21%)
    all_to_all x2, blocking collectives, exchange(): lax.all_to_all(blocks, AXES, split_axis=0, concat_axis=0, tiled=True)  62.1 us
    pallas_call x1, Pallas kernels, update(): pl.pallas_call(update_kernel, out_shape=(jax.ShapeDtypeStruct((width, row...  11.7 us
    pallas_call x1, Pallas kernels, pack(): pl.pallas_call(functools.partial(pack_kernel, owners, cap), out_shape=(se...  3.01 us
    pallas_call x1, Pallas kernels, unpack(): pl.pallas_call(functools.partial(unpack_kernel, cap), out_shape=(jax.Shap...  2.33 us

profile of v5, /device:TPU:1, one launch (start us, length us, event | category | flops | bytes accessed | tf_op | source)
XLA Modules:
  0.0 79.8 jit_solution(8864938045924619081)
XLA Ops:
  0.6 0.0 copy-start
  0.6 3.0 %pack.1 = (bf16[2048,384]{1,0:T(8,128)(2,1)S(1)}, s32[1,1024]{1,0:T(1,128)S(1)}) custom-call(s32[1,1024]{1,0:T(1,128)} %bitcast.21, s32[1,1024]{1,0:T(1,128)} %bitcast.22, bf16[320,1024]{1,0:T(8,128)(2,1)} %bitcast.19), custom_call_target="tpu_custom_call" | custom-call | flops 1610612736 | bytes 2236416 | tf_op jit(solution)/shard_map/pack/pallas_call | solution.py:192
  3.7 0.0 copy-start.1
  3.7 36.0 %all_to_all.10 = bf16[128,16,384]{2,1,0:T(8,128)(2,1)S(1)} all-to-all(bf16[128,16,384]{2,1,0:T(8,128)(2,1)S(1)} %bitcast.14), channel_id=1, replica_groups=mesh['gx'=4,'gy'=4,'gz'=8] {'gx','gy','gz'}, dimensions={0} | all-to-all | bytes 3145728 | tf_op jit(solution)/shard_map/all_to_all | solution.py:266
  39.7 0.0 copy-done
  39.7 0.0 copy-done.1
  39.7 11.7 %update.1 = (f32[320,4096]{1,0:T(8,128)}, f32[320,2048]{1,0:T(8,128)S(1)}, f32[1,4096]{1,0:T(1,128)}, bf16[1024,640]{1,0:T(8,128)(2,1)S(1)}) custom-call(bf16[2048,384]{1,0:T(8,128)(2,1)S(1)} %bitcast.13, f32[1,4096]{1,0:T(1,128)S(1)} %bitcast.17, f32[320,4096]{1,0:T(8,128)S(1)} %bitcast.16), custom_call_target="tpu_custom_call" | custom-call | flops 10737418240 | bytes 12075008 | tf_op jit(solution)/shard_map/update/pallas_call | solution.py:216
  51.4 26.1 %all_to_all.11 = bf16[128,8,640]{2,1,0:T(8,128)(2,1)S(1)} all-to-all(bf16[128,8,640]{2,1,0:T(8,128)(2,1)S(1)} %bitcast.15), channel_id=1, replica_groups=mesh['gx'=4,'gy'=4,'gz'=8] {'gx','gy','gz'}, dimensions={0} | all-to-all | bytes 2621440 | tf_op jit(solution)/shard_map/all_to_all | solution.py:266
  77.4 2.3 %unpack.1 = (bf16[320,1024]{1,0:T(8,128)(2,1)}, f32[320,4096]{1,0:T(8,128)}) custom-call(bf16[1024,640]{1,0:T(8,128)(2,1)S(1)} %bitcast.12, s32[1,1024]{1,0:T(1,128)S(1)} %get-tuple-element.13.target_ref, f32[320,2048]{1,0:T(8,128)S(1)} %get-tuple-element.14.rest_ref, f32[320,4096]{1,0:T(8,128)} %get-tuple-element.15.part_hbm), custom_call_target="tpu_custom_call", output_to_operand_aliasing={{1}: (3, {})} | custom-call | flops 1342177280 | bytes 6553600 | tf_op jit(solution)/shard_map/unpack/pallas_call | solution.py:243
Async XLA Ops:
  0.6 39.0 %copy-start = (f32[4096,320]{0,1:T(8,128)S(1)}, f32[4096,320]{0,1:T(8,128)}, u32[]{:S(2)}) copy-start(f32[4096,320]{0,1:T(8,128)} %param.8) | copy-start | bytes 15728644
  3.7 36.0 %copy-start.1 = (f32[4096]{0:T(1024)S(1)}, f32[4096]{0:T(1024)}, u32[]{:S(2)}) copy-start(f32[4096]{0:T(1024)} %param.9) | copy-start | bytes 49156

commit v6 on v5

--- a/solution.py
+++ b/solution.py
@@ -108,24 +108,36 @@
             rest_ref[...] = moved
         rounded_ref[:, part] = moved.astype(jnp.bfloat16)
 
+    step = min(512, slots)
+
+    def picked_of(first, last, b):
+        below = lax.broadcasted_iota(jnp.int16, (last - first, step), 0)
+        wanted = row_across[:, b * step : (b + 1) * step] - jnp.int16(first)
+        onehot = jnp.where(below == wanted, one, zero)
+        return jnp.dot(
+            rounded_ref[:, first:last], onehot, preferred_element_type=jnp.float32
+        )
+
+    early = rows - tile
     ahead = summed_of(0)
     for j in range(tiles):
         summed = ahead
         if j + 1 < tiles:
             ahead = summed_of(j + 1)
+        elif early:
+            begun = picked_of(0, early, 0)
         settle(j, summed)
     grown_copy = pltpu.make_async_copy(grown_ref, grown_hbm, sem)
     grown_copy.start()
-    early = rows - tile
     copies = copies_of(new_ref, new_hbm.at[:, 0:early], new_sem)
     for copy in copies:
         copy.start()
 
-    step = min(512, slots)
-    below = lax.broadcasted_iota(jnp.int16, (rows, step), 0)
     for b in range(slots // step):
-        onehot = jnp.where(below == row_across[:, b * step : (b + 1) * step], one, zero)
-        picked = jnp.dot(rounded_ref[...], onehot, preferred_element_type=jnp.float32)
+        if b == 0 and early:
+            picked = begun + picked_of(early, rows, b)
+        else:
+            picked = picked_of(0, rows, b)
         picked = picked.T.reshape(step // 16, 2, 8, width)
         lower = picked[:, 0].reshape(step // 2, width)
         upper = picked[:, 1].reshape(step // 2, width)
@@ -159,10 +171,10 @@
     turned = back_ref[...].T
     turned_ref[:, 0:half] = turned[0:width]
     turned_ref[:, half:] = turned[width:]
-    step = tokens // 2
-    place = lax.broadcasted_iota(jnp.int16, (2 * half, step), 0)
-    for b in range(2):
-        part = slice(b * step, (b + 1) * step)
+    edges = [0, tokens // 2, 3 * tokens // 4, tokens]
+    for b in range(3):
+        part = slice(edges[b], edges[b + 1])
+        place = lax.broadcasted_iota(jnp.int16, (2 * half, edges[b + 1] - edges[b]), 0)
         onehot = jnp.where(place == spot[:, part], jnp.bfloat16(1), jnp.bfloat16(0))
         fresh_ref[:, part] = jnp.dot(
             turned_ref[...], onehot, preferred_element_type=jnp.float32
@@ -252,7 +264,7 @@
         scratch_shapes=[
             pltpu.VMEM((width, 2 * back.shape[0]), jnp.bfloat16),
             pltpu.VMEM((width, tokens), jnp.bfloat16),
-            pltpu.SemaphoreType.DMA((2,)),
+            pltpu.SemaphoreType.DMA((3,)),
             pltpu.SemaphoreType.DMA((4,)),
         ],
         compiler_params=pltpu.CompilerParams(vmem_limit_bytes=LIMIT),

time: 80 us -> 79.9 us (level)
  no operation moved by 1% of the time
where the time goes in v6:
time: 79.9 us; the launch traced here: 79.7 us
  blocking collectives  62.1 us (78%)
  Pallas kernels  17 us (21%)
    all_to_all x2, blocking collectives, exchange(): lax.all_to_all(blocks, AXES, split_axis=0, concat_axis=0, tiled=True)  62.1 us
    pallas_call x1, Pallas kernels, update(): pl.pallas_call(update_kernel, out_shape=(jax.ShapeDtypeStruct((width, row...  11.6 us
    pallas_call x1, Pallas kernels, pack(): pl.pallas_call(functools.partial(pack_kernel, owners, cap), out_shape=(se...  3.01 us
    pallas_call x1, Pallas kernels, unpack(): pl.pallas_call(functools.partial(unpack_kernel, cap), out_shape=(jax.Shap...  2.34 us

profile of v6, /device:TPU:1, one launch (start us, length us, event | category | flops | bytes accessed | tf_op | source)
XLA Modules:
  0.0 79.7 jit_solution(14472045753753202684)
XLA Ops:
  0.6 0.0 copy-start
  0.6 3.0 %pack.1 = (bf16[2048,384]{1,0:T(8,128)(2,1)S(1)}, s32[1,1024]{1,0:T(1,128)S(1)}) custom-call(s32[1,1024]{1,0:T(1,128)} %bitcast.21, s32[1,1024]{1,0:T(1,128)} %bitcast.22, bf16[320,1024]{1,0:T(8,128)(2,1)} %bitcast.19), custom_call_target="tpu_custom_call" | custom-call | flops 1610612736 | bytes 2236416 | tf_op jit(solution)/shard_map/pack/pallas_call | solution.py:204
  3.7 0.0 copy-start.1
  3.7 36.0 %all_to_all.10 = bf16[128,16,384]{2,1,0:T(8,128)(2,1)S(1)} all-to-all(bf16[128,16,384]{2,1,0:T(8,128)(2,1)S(1)} %bitcast.14), channel_id=1, replica_groups=mesh['gx'=4,'gy'=4,'gz'=8] {'gx','gy','gz'}, dimensions={0} | all-to-all | bytes 3145728 | tf_op jit(solution)/shard_map/all_to_all | solution.py:278
  39.7 0.0 copy-done
  39.7 0.0 copy-done.1
  39.7 11.6 %update.1 = (f32[320,4096]{1,0:T(8,128)}, f32[320,2048]{1,0:T(8,128)S(1)}, f32[1,4096]{1,0:T(1,128)}, bf16[1024,640]{1,0:T(8,128)(2,1)S(1)}) custom-call(bf16[2048,384]{1,0:T(8,128)(2,1)S(1)} %bitcast.13, f32[1,4096]{1,0:T(1,128)S(1)} %bitcast.17, f32[320,4096]{1,0:T(8,128)S(1)} %bitcast.16), custom_call_target="tpu_custom_call" | custom-call | flops 10737418240 | bytes 12075008 | tf_op jit(solution)/shard_map/update/pallas_call | solution.py:228
  51.3 26.1 %all_to_all.11 = bf16[128,8,640]{2,1,0:T(8,128)(2,1)S(1)} all-to-all(bf16[128,8,640]{2,1,0:T(8,128)(2,1)S(1)} %bitcast.15), channel_id=1, replica_groups=mesh['gx'=4,'gy'=4,'gz'=8] {'gx','gy','gz'}, dimensions={0} | all-to-all | bytes 2621440 | tf_op jit(solution)/shard_map/all_to_all | solution.py:278
  77.4 2.3 %unpack.1 = (bf16[320,1024]{1,0:T(8,128)(2,1)}, f32[320,4096]{1,0:T(8,128)}) custom-call(bf16[1024,640]{1,0:T(8,128)(2,1)S(1)} %bitcast.12, s32[1,1024]{1,0:T(1,128)S(1)} %get-tuple-element.13.target_ref, f32[320,2048]{1,0:T(8,128)S(1)} %get-tuple-element.14.rest_ref, f32[320,4096]{1,0:T(8,128)} %get-tuple-element.15.part_hbm), custom_call_target="tpu_custom_call", output_to_operand_aliasing={{1}: (3, {})} | custom-call | flops 1342177280 | bytes 6553600 | tf_op jit(solution)/shard_map/unpack/pallas_call | solution.py:255
Async XLA Ops:
  0.6 39.0 %copy-start = (f32[4096,320]{0,1:T(8,128)S(1)}, f32[4096,320]{0,1:T(8,128)}, u32[]{:S(2)}) copy-start(f32[4096,320]{0,1:T(8,128)} %param.8) | copy-start | bytes 15728644
  3.7 36.0 %copy-start.1 = (f32[4096]{0:T(1024)S(1)}, f32[4096]{0:T(1024)}, u32[]{:S(2)}) copy-start(f32[4096]{0:T(1024)} %param.9) | copy-start | bytes 49156
